TPU v7x, 128 devices: a whole 4x4x4 slice. The times are simulated.
128 devices in a mesh: dp: 4 (over x), expert: 32 (over z, y, core).
Axes of the slice: x: 4, y: 4, z: 4, core: 2. Of those that a mesh axis runs over, the one named last changes fastest.
Arguments:
- tokens: bfloat16 [16384, 7168], P('expert', 'dp'), may hold values from -6 to 6
- grad_out: bfloat16 [16384, 7168], P('expert', 'dp'), may hold values from -6 to 6
- route_ids: int32 [16384, 1], P('expert'), may hold values from 0 to 31; in each aligned block of 512 rows (0 to 511, 512 to 1023, ...) at most 20 rows name the same one
- gate_codes: int32 [16384, 1], P('expert'), may hold values from 1 to 255
- gate_weight: bfloat16 [32, 7168, 1024], P('expert', 'dp'), may hold values from -0.0625 to 0.0625
- up_weight: bfloat16 [32, 7168, 1024], P('expert', 'dp'), may hold values from -0.0625 to 0.0625
- down_weight: bfloat16 [32, 1024, 7168], P('expert', None, 'dp'), may hold values from -0.1875 to 0.1875
- momentum: bfloat16 [32, 1024, 7168], P('expert', None, 'dp'), may hold values from -6 to 6
Outputs:
- grad_tokens: bfloat16 [16384, 7168], P('expert', 'dp')
- new_down: bfloat16 [32, 1024, 7168], P('expert', None, 'dp')
- new_momentum: bfloat16 [32, 1024, 7168], P('expert', None, 'dp')
Inputs may be any that keep to these rules, and one draw needn't show every extreme that they name: `route_ids`: each token names one expert. Among the 512 tokens of one index of the expert axis no expert is named by more than 20 tokens, a bound that some block reaches.
All inputs are finite; a program needn't handle non-finite values.
Results may differ from a plain program's by a relative error of at most 0.022.
Values may be sent and summed in bfloat16 or wider, within the bound.
A program may use at most 128 MiB of HBM per device.

v0:
```python
import jax
import jax.numpy as jnp
from jax import lax
from jax.sharding import PartitionSpec as P

first_beta = 0.9
second_beta = 0.9
learn_rate = 0.01
decay_rate = 3.0
soft_width = 1.0


def activate(terms):
    pre_gate = terms[:, 0, :]
    pre_up = terms[:, 1, :]
    grad_hidden = terms[:, 2, :]
    sigmoid = jax.nn.sigmoid(pre_gate)
    active = pre_gate * sigmoid
    hidden = (active * pre_up).astype(jnp.bfloat16)
    d_gate = (grad_hidden * pre_up * sigmoid * (1.0 + pre_gate * (1.0 - sigmoid))).astype(
        jnp.bfloat16
    )
    d_up = (grad_hidden * active).astype(jnp.bfloat16)
    return (hidden, d_gate, d_up)


def contract_last(left, right):
    return lax.dot_general(
        left, right, (((1,), (1,)), ((), ())), preferred_element_type=jnp.float32
    )


def contract_first(left, right):
    return lax.dot_general(
        left, right, (((0,), (0,)), ((), ())), preferred_element_type=jnp.float32
    )


def local(tokens, grad_out, route_ids, gate_codes, gate_weight, up_weight, down_weight, momentum):
    n_expert = lax.axis_size("expert")
    tok_rows, slab = tokens.shape
    top = route_ids.shape[1]
    capacity = max(2, tok_rows * top * 5 // (4 * n_expert))
    flat_ids = route_ids.reshape(-1)
    expert_iota = jnp.arange(n_expert, dtype=jnp.int32)
    onehot = (flat_ids[:, None] == expert_iota[None, :]).astype(jnp.int32)
    before = jnp.cumsum(onehot, axis=0) - onehot
    slot = jnp.sum(before * onehot, axis=1)
    target = flat_ids * capacity + slot
    slot_iota = jnp.arange(n_expert * capacity, dtype=jnp.int32)
    placed = (
        (target[None, :] == slot_iota[:, None])
        .astype(jnp.float32)
        .reshape(n_expert * capacity, tok_rows, top)
    )
    route_scale = gate_codes.astype(jnp.float32) / 256.0
    picker = jnp.sum(placed, axis=2).astype(jnp.bfloat16)
    scaler = jnp.sum(placed * route_scale[None, :, :], axis=2).astype(jnp.bfloat16)
    send_x = jnp.dot(picker, tokens, preferred_element_type=jnp.float32).astype(jnp.bfloat16)
    send_dy = jnp.dot(scaler, grad_out, preferred_element_type=jnp.float32).astype(jnp.bfloat16)
    send_x = send_x.reshape(n_expert, capacity, slab)
    send_dy = send_dy.reshape(n_expert, capacity, slab)
    recv_x, recv_dy = (
        lax.all_to_all(send_x, "expert", split_axis=0, concat_axis=0, tiled=True),
        lax.all_to_all(send_dy, "expert", split_axis=0, concat_axis=0, tiled=True),
    )
    x_rows = recv_x.reshape(-1, slab)
    dy_rows = recv_dy.reshape(-1, slab)
    w_gate = gate_weight[0]
    w_up = up_weight[0]
    w_down = down_weight[0]
    dy_part = dy_rows
    gate_part = jnp.dot(x_rows, w_gate, preferred_element_type=jnp.float32)
    up_part = jnp.dot(x_rows, w_up, preferred_element_type=jnp.float32)
    back_part = contract_last(dy_part, w_down)
    shares = lax.psum_scatter(
        jnp.stack([gate_part, up_part, back_part], axis=1).astype(jnp.bfloat16),
        "dp",
        scatter_dimension=0,
        tiled=True,
    ).astype(jnp.float32)
    hidden, d_gate, d_up = activate(shares)
    hidden_part = lax.all_gather(hidden, "dp", axis=0, tiled=True)
    gate_part = lax.all_gather(d_gate, "dp", axis=0, tiled=True)
    up_part = lax.all_gather(d_up, "dp", axis=0, tiled=True)
    dy_part = dy_rows
    grad_w = contract_first(hidden_part, dy_part)
    rows_x = contract_last(gate_part, w_gate) + contract_last(up_part, w_up)
    grad_x = rows_x
    grad_down, grad_x = (grad_w, grad_x)
    back = grad_x.astype(jnp.bfloat16).reshape(n_expert, capacity, slab)
    returned = lax.all_to_all(back, "expert", split_axis=0, concat_axis=0, tiled=True)
    returned = returned.reshape(n_expert * capacity, slab)
    grad_tokens = contract_first(picker, returned).astype(jnp.bfloat16)
    moment = momentum[0].astype(jnp.float32)
    weight = w_down.astype(jnp.float32)
    blend = first_beta * moment + (1.0 - first_beta) * grad_down
    step = blend / jnp.sqrt(blend * blend + soft_width * soft_width)
    agree = jnp.maximum(step * jnp.sign(weight), 0.0)
    new_down = (weight - learn_rate * (step + decay_rate * agree * weight)).astype(jnp.bfloat16)
    new_moment = (second_beta * moment + (1.0 - second_beta) * grad_down).astype(jnp.bfloat16)
    return (grad_tokens, new_down[None], new_moment[None])


def solution(mesh):
    placed = (
        P("expert", "dp"),
        P("expert", "dp"),
        P("expert", None),
        P("expert", None),
        P("expert", "dp", None),
        P("expert", "dp", None),
        P("expert", None, "dp"),
        P("expert", None, "dp"),
    )
    return jax.shard_map(
        local,
        mesh=mesh,
        in_specs=placed,
        out_specs=(P("expert", "dp"), P("expert", None, "dp"), P("expert", None, "dp")),
        check_vma=False,
    )
```

profile of v0, /device:TPU:0, one launch (start us, length us, event | category | flops | bytes accessed | tf_op | source)
XLA Modules:
  0.0 284.5 jit_solution(3125101756731378622)
XLA Ops:
  7.2 0.8 fusion.48
  8.0 1.2 reduce-window.6
  9.4 0.8 fusion.47
  10.2 0.7 multiply_add_fusion
  10.9 2.7 convolution_convert_fusion.1
  13.6 4.1 %reshape.132 = bf16[32,20,1792]{2,1,0:T(8,128)(2,1)} reshape(bf16[640,1792]{1,0:T(8,128)(2,1)} %convolution_convert_fusion.1) | data formatting | bytes 4587520 | tf_op jit(solution)/shard_map/reshape | solution.py:61
  17.7 8.5 %all-to-all-start = ((bf16[32,20,1792]{2,1,0:T(8,128)(2,1)}), bf16[32,20,1792]{2,1,0:T(8,128)(2,1)S(1)}, u32[]{:S(2)}, u32[]{:S(2)}) async-start(bf16[32,20,1792]{2,1,0:T(8,128)(2,1)} %reshape.132), calls=%async_computation | async-start | bytes 5505024 | tf_op jit(solution)/shard_map/all_to_all | solution.py:64
  26.3 4.3 %convolution_convert_fusion = bf16[640,1792]{1,0:T(8,128)(2,1)} fusion(bf16[512,1792]{1,0:T(8,128)(2,1)} %param.9, f32[512]{0:T(512)S(1)} %bitcast.104, s32[512]{0:T(512)S(1)} %multiply_add_fusion), kind=kOutput, calls=%fused_computation.24 | convolution fusion | flops 1176207360 | bytes 4132864 | tf_op jit(solution)/shard_map/dot_general | solution.py:60
  30.6 4.1 %reshape.134 = bf16[32,20,1792]{2,1,0:T(8,128)(2,1)} reshape(bf16[640,1792]{1,0:T(8,128)(2,1)} %convolution_convert_fusion) | data formatting | bytes 4587520 | tf_op jit(solution)/shard_map/reshape | solution.py:62
  34.7 29.1 %all-to-all-done = bf16[32,20,1792]{2,1,0:T(8,128)(2,1)S(1)} async-done(((bf16[32,20,1792]{2,1,0:T(8,128)(2,1)}), bf16[32,20,1792]{2,1,0:T(8,128)(2,1)S(1)}, u32[]{:S(2)}, u32[]{:S(2)}) %all-to-all-start) | async-done | bytes 2293792 | tf_op jit(solution)/shard_map/all_to_all | solution.py:64
  63.8 4.8 %all-to-all-start.1 = ((bf16[32,20,1792]{2,1,0:T(8,128)(2,1)}), bf16[32,20,1792]{2,1,0:T(8,128)(2,1)}, u32[]{:S(2)}, u32[]{:S(2)}) async-start(bf16[32,20,1792]{2,1,0:T(8,128)(2,1)} %reshape.134), calls=%async_computation.1 | async-start | bytes 5505024 | tf_op jit(solution)/shard_map/all_to_all | solution.py:65
  68.6 2.1 reshape.133
  70.7 6.5 %fusion.31 = bf16[640,1,1024]{2,0,1:T(8,128)(2,1)} fusion(bf16[640,1792]{1,0:T(8,128)(2,1)} %reshape.133, bf16[1,1792,1024]{2,1,0:T(8,128)(2,1)} %param.13), kind=kOutput, calls=%fused_computation.31 | convolution fusion | flops 2349465600 | bytes 7274496 | tf_op jit(solution)/shard_map/dot_general | solution.py:74
  77.2 3.6 %fusion.34 = bf16[640,1,1024]{2,0,1:T(8,128)(2,1)} fusion(bf16[640,1792]{1,0:T(8,128)(2,1)S(1)} %copy-done.2, bf16[1,1792,1024]{2,1,0:T(8,128)(2,1)S(1)} %copy-done.6), kind=kOutput, calls=%fused_computation.32 | convolution fusion | flops 2349465600 | bytes 7274496 | tf_op jit(solution)/shard_map/dot_general | solution.py:73
  80.8 25.3 %all-to-all-done.1 = bf16[32,20,1792]{2,1,0:T(8,128)(2,1)} async-done(((bf16[32,20,1792]{2,1,0:T(8,128)(2,1)}), bf16[32,20,1792]{2,1,0:T(8,128)(2,1)}, u32[]{:S(2)}, u32[]{:S(2)}) %all-to-all-start.1) | async-done | bytes 2293792 | tf_op jit(solution)/shard_map/all_to_all | solution.py:65
  106.1 2.7 reshape.135
  108.8 4.8 %fusion.28 = bf16[640,1,1024]{2,0,1:T(8,128)(2,1)S(1)} fusion(bf16[640,1792]{1,0:T(8,128)(2,1)S(1)} %reshape.135, bf16[1,1024,1792]{2,1,0:T(8,128)(2,1)} %param.14), kind=kOutput, calls=%fused_computation.30 | convolution fusion | flops 2349465600 | bytes 7274496 | tf_op jit(solution)/shard_map/dot_general | solution.py:28
  113.6 2.1 pad_maximum_fusion
  115.8 41.3 %reduce-scatter.2.cloned.1.call-done = bf16[160,3,1024]{2,0,1:T(8,128)(2,1)} async-done(((bf16[640,3,1024]{2,0,1:T(8,128)(2,1)}), bf16[160,3,1024]{2,0,1:T(8,128)(2,1)}) %reduce-scatter.2.cloned.1.call-update) | async-done | bytes 983056 | tf_op jit(solution)/shard_map/reduce_scatter | solution.py:76
  157.1 1.4 convert_element_type.104
  158.5 1.4 multiply_convert_fusion
  161.2 23.5 %all-gather.6.cloned.1.call-done = bf16[640,1024]{1,0:T(8,128)(2,1)} async-done(((bf16[160,1024]{1,0:T(8,128)(2,1)}), bf16[640,1024]{1,0:T(8,128)(2,1)}) %all-gather.6.cloned.1.call-update) | async-done | bytes 1310736 | tf_op jit(solution)/shard_map/all_gather | solution.py:85
  184.7 7.1 %fusion.8 = f32[640,1792]{1,0:T(8,128)} fusion(bf16[640,1024]{1,0:T(8,128)(2,1)} %all-gather.6.cloned.1.call-done, bf16[1,1792,1024]{2,1,0:T(8,128)(2,1)} %param.13), kind=kOutput, calls=%fused_computation.14 | convolution fusion | flops 2348810240 | bytes 9568256 | tf_op jit(solution)/shard_map/dot_general | solution.py:28
  191.8 20.6 %all-gather.4.cloned.1.call-done = bf16[640,1024]{1,0:T(8,128)(2,1)} async-done(((bf16[160,1024]{1,0:T(8,128)(2,1)}), bf16[640,1024]{1,0:T(8,128)(2,1)}) %all-gather.4.cloned.1.call-update) | async-done | bytes 1310736 | tf_op jit(solution)/shard_map/all_gather | solution.py:84
  212.4 7.8 %add_convert_fusion = bf16[640,1792]{1,0:T(8,128)(2,1)} fusion(f32[640,1792]{1,0:T(8,128)} %fusion.8, bf16[640,1024]{1,0:T(8,128)(2,1)} %all-gather.4.cloned.1.call-done, bf16[1,1792,1024]{2,1,0:T(8,128)(2,1)} %param.12), kind=kOutput, calls=%fused_computation.10 | convolution fusion | flops 2351104000 | bytes 11862016 | tf_op jit(solution)/shard_map/dot_general | solution.py:28
  220.2 4.1 %reshape.136 = bf16[32,20,1792]{2,1,0:T(8,128)(2,1)} reshape(bf16[640,1792]{1,0:T(8,128)(2,1)} %add_convert_fusion) | data formatting | bytes 4587520 | tf_op jit(solution)/shard_map/reshape | solution.py:91
  224.3 7.4 %all-to-all-start.2 = ((bf16[32,20,1792]{2,1,0:T(8,128)(2,1)}), bf16[32,20,1792]{2,1,0:T(8,128)(2,1)}, u32[]{:S(2)}, u32[]{:S(2)}) async-start(bf16[32,20,1792]{2,1,0:T(8,128)(2,1)} %reshape.136), calls=%async_computation.3 | async-start | bytes 5505024 | tf_op jit(solution)/shard_map/all_to_all | solution.py:92
  231.7 8.3 %all-gather.8.cloned.1.call-done = bf16[640,1024]{1,0:T(8,128)(2,1)} async-done(((bf16[160,1024]{1,0:T(8,128)(2,1)}), bf16[640,1024]{1,0:T(8,128)(2,1)}) %all-gather.8.cloned.1.call-update) | async-done | bytes 1310736 | tf_op jit(solution)/shard_map/all_gather | solution.py:83
  240.0 12.7 %convert_bitcast_fusion = (bf16[1,1024,1792]{2,1,0:T(8,128)(2,1)}, bf16[1,1024,1792]{2,1,0:T(8,128)(2,1)}) fusion(bf16[1,1024,1792]{2,1,0:T(8,128)(2,1)} %param.14, bf16[640,1024]{1,0:T(8,128)(2,1)} %all-gather.8.cloned.1.call-done, bf16[640,1792]{1,0:T(8,128)(2,1)S(1)} %reshape.135, bf16[1,1024,1792]{2,1,0:T(8,128)(2,1)} %param.15), kind=kOutput, calls=%fused_computation.22 | convolution fusion | flops 2381840384 | bytes 18284544 | tf_op jit(solution)/shard_map/dot_general | solution.py:34
  252.7 16.5 %all-to-all-done.2 = bf16[32,20,1792]{2,1,0:T(8,128)(2,1)} async-done(((bf16[32,20,1792]{2,1,0:T(8,128)(2,1)}), bf16[32,20,1792]{2,1,0:T(8,128)(2,1)}, u32[]{:S(2)}, u32[]{:S(2)}) %all-to-all-start.2) | async-done | bytes 2293792 | tf_op jit(solution)/shard_map/all_to_all | solution.py:92
  269.1 4.3 %reshape.137 = bf16[640,1792]{1,0:T(8,128)(2,1)} reshape(bf16[32,20,1792]{2,1,0:T(8,128)(2,1)} %all-to-all-done.2) | data formatting | bytes 4587520 | tf_op jit(solution)/shard_map/reshape | solution.py:93
  273.4 4.5 %convolution_convert_fusion.2 = bf16[512,1792]{1,0:T(8,128)(2,1)} fusion(bf16[640,1792]{1,0:T(8,128)(2,1)} %reshape.137, s32[512]{0:T(512)S(1)} %multiply_add_fusion), kind=kOutput, calls=%fused_computation.26 | convolution fusion | flops 1176305664 | bytes 4130816 | tf_op jit(solution)/shard_map/dot_general | solution.py:34
  (26 shorter events, 1.7 us)
Async XLA Ops:
  7.2 3.7 %copy-start = (bf16[512,1792]{1,0:T(8,128)(2,1)S(1)}, bf16[512,1792]{1,0:T(8,128)(2,1)}, u32[]{:S(2)}) copy-start(bf16[512,1792]{1,0:T(8,128)(2,1)} %param.8) | copy-start | bytes 5505028
  17.7 8.6 %copy-start.5 = (s32[512,1]{0,1:T(1,128)S(1)}, s32[512,1]{0,1:T(1,128)}, u32[]{:S(2)}) copy-start(s32[512,1]{0,1:T(1,128)} %param.11) | copy-start | bytes 6148
  17.7 46.0 %all-to-all-start = ((bf16[32,20,1792]{2,1,0:T(8,128)(2,1)}), bf16[32,20,1792]{2,1,0:T(8,128)(2,1)S(1)}, u32[]{:S(2)}, u32[]{:S(2)}) async-start(bf16[32,20,1792]{2,1,0:T(8,128)(2,1)} %reshape.132), calls=%async_computation | async-start | bytes 5505024 | tf_op jit(solution)/shard_map/all_to_all | solution.py:64
  63.8 42.3 %all-to-all-start.1 = ((bf16[32,20,1792]{2,1,0:T(8,128)(2,1)}), bf16[32,20,1792]{2,1,0:T(8,128)(2,1)}, u32[]{:S(2)}, u32[]{:S(2)}) async-start(bf16[32,20,1792]{2,1,0:T(8,128)(2,1)} %reshape.134), calls=%async_computation.1 | async-start | bytes 5505024 | tf_op jit(solution)/shard_map/all_to_all | solution.py:65
  68.6 88.5 %reduce-scatter.2.cloned.1.call-start = ((), (), s32[]{:S(2)}) async-start(), calls=%async_computation.4 | async-start | bytes 4915200 | tf_op jit(solution)/shard_map/reduce_scatter | solution.py:76
  70.7 6.5 %copy-start.2 = (bf16[640,1792]{1,0:T(8,128)(2,1)S(1)}, bf16[640,1792]{1,0:T(8,128)(2,1)}, u32[]{:S(2)}) copy-start(bf16[640,1792]{1,0:T(8,128)(2,1)} %reshape.133) | copy-start | bytes 6881284
  70.7 6.5 %copy-start.6 = (bf16[1,1792,1024]{2,1,0:T(8,128)(2,1)S(1)}, bf16[1,1792,1024]{2,1,0:T(8,128)(2,1)}, u32[]{:S(2)}) copy-start(bf16[1,1792,1024]{2,1,0:T(8,128)(2,1)} %param.12) | copy-start | bytes 11010052
  108.8 4.8 %copy-start.3 = (bf16[640,1,1024]{2,0,1:T(8,128)(2,1)S(1)}, bf16[640,1,1024]{2,0,1:T(8,128)(2,1)}, u32[]{:S(2)}) copy-start(bf16[640,1,1024]{2,0,1:T(8,128)(2,1)} %fusion.31) | copy-start | bytes 3932164
  108.8 4.8 %copy-start.4 = (bf16[640,1,1024]{2,0,1:T(8,128)(2,1)S(1)}, bf16[640,1,1024]{2,0,1:T(8,128)(2,1)}, u32[]{:S(2)}) copy-start(bf16[640,1,1024]{2,0,1:T(8,128)(2,1)} %fusion.34) | copy-start | bytes 3932164
  115.7 69.0 %all-gather.6.cloned.1.call-start = ((), (), s32[]{:S(2)}) async-start(), calls=%async_computation.6 | async-start | bytes 1638400 | tf_op jit(solution)/shard_map/all_gather | solution.py:85
  159.9 52.5 %all-gather.4.cloned.1.call-start = ((), (), s32[]{:S(2)}) async-start(), calls=%async_computation.5 | async-start | bytes 1638400 | tf_op jit(solution)/shard_map/all_gather | solution.py:84
  160.6 79.4 %all-gather.8.cloned.1.call-start = ((), (), s32[]{:S(2)}) async-start(), calls=%async_computation.7 | async-start | bytes 1638400 | tf_op jit(solution)/shard_map/all_gather | solution.py:83
  224.3 44.8 %all-to-all-start.2 = ((bf16[32,20,1792]{2,1,0:T(8,128)(2,1)}), bf16[32,20,1792]{2,1,0:T(8,128)(2,1)}, u32[]{:S(2)}, u32[]{:S(2)}) async-start(bf16[32,20,1792]{2,1,0:T(8,128)(2,1)} %reshape.136), calls=%async_computation.3 | async-start | bytes 5505024 | tf_op jit(solution)/shard_map/all_to_all | solution.py:92
  269.1 8.8 %copy-start.1 = (bf16[512,1792]{1,0:T(8,128)(2,1)S(1)}, bf16[512,1792]{1,0:T(8,128)(2,1)}, u32[]{:S(2)}) copy-start(bf16[512,1792]{1,0:T(8,128)(2,1)} %param.8) | copy-start | bytes 5505028
Sparse Core Ops, SparseCore 0:
  115.8 41.1 reduce-scatter.1
  160.0 24.6 all-gather.5
  186.9 25.4 all-gather.3
  214.5 25.4 all-gather.7
where the time goes:
time: 285 us; the launch traced here: 284 us
  waiting for transfers between devices  166 us (58%)
  matrix products  53.9 us (19%)
  local copies, waits for them, and re-layouts  21.6 us (8%)
  starting transfers between devices  21.1 us (7%)
  between operations  13.9 us (5%)
  other arithmetic  8.4 us (3%)
    reduce_scatter x1, waiting for transfers between devices, local(): lax.psum_scatter(jnp.stack([gate_part, up_part, back_part], axis=1).astyp...  41.3 us
    all_to_all x1, waiting for transfers between devices, local(): lax.all_to_all(send_x, 'expert', split_axis=0, concat_axis=0, tiled=True)  29.1 us
    all_to_all x1, waiting for transfers between devices, local(): lax.all_to_all(send_dy, 'expert', split_axis=0, concat_axis=0, tiled=True)  25.3 us
    all_gather x1, waiting for transfers between devices, local(): up_part = lax.all_gather(d_up, 'dp', axis=0, tiled=True)  23.5 us
    all_gather x1, waiting for transfers between devices, local(): gate_part = lax.all_gather(d_gate, 'dp', axis=0, tiled=True)  20.6 us
    dot_general x3, matrix products, contract_last(): lax.dot_general(left, right, (((1,), (1,)), ((), ())), preferred_element_...  19.6 us
    dot_general x2, matrix products, contract_first(): lax.dot_general(left, right, (((0,), (0,)), ((), ())), preferred_element_...  17.2 us
    all_to_all x1, waiting for transfers between devices, local(): lax.all_to_all(back, 'expert', split_axis=0, concat_axis=0, tiled=True)  16.5 us
  transfers between devices with their start and end apart: 7, of which 7 were waited for; matrix products, arithmetic and copies ran while one was open for 18% of the time, Pallas kernels for 0%

commit v1 on v0

--- a/solution.py
+++ b/solution.py
@@ -80,8 +80,11 @@
         tiled=True,
     ).astype(jnp.float32)
     hidden, d_gate, d_up = activate(shares)
-    hidden_part = lax.all_gather(hidden, "dp", axis=0, tiled=True)
-    gate_part = lax.all_gather(d_gate, "dp", axis=0, tiled=True)
+    hidden_part, gate_part = jnp.split(
+        lax.all_gather(jnp.concatenate([hidden, d_gate], axis=1), "dp", axis=0, tiled=True),
+        [hidden.shape[1]],
+        axis=1,
+    )
     up_part = lax.all_gather(d_up, "dp", axis=0, tiled=True)
     dy_part = dy_rows
     grad_w = contract_first(hidden_part, dy_part)

time: 285 us -> 295 us (1.035)
  waiting for transfers between devices: 166 us -> 175 us
    all_to_all x1, waiting for transfers between devices: 16.5 us -> 24.8 us  [local(): lax.all_to_all(back, 'expert', split_axis=0, concat_axis=0, tiled=True)]
    all_gather x2 -> x1, waiting for transfers between devices: 29 us -> 30.9 us  [local(): lax.all_gather(jnp.concatenate([hidden, d_gate], axis=1), 'dp', axis=0, t...]
  transfers between devices with their start and end apart: 7 -> 6, of which waited for: 7 -> 6; matrix products, arithmetic and copies ran while one was open for 18% -> 14% of each run, Pallas kernels for 0% -> 0%
where the time goes in v1:
time: 295 us
  waiting for transfers between devices  175 us (59%)
  matrix products  53.9 us (18%)
  local copies, waits for them, and re-layouts  21.6 us (7%)
  starting transfers between devices  21 us (7%)
  between operations  13.9 us (5%)
  other arithmetic  9.08 us (3%)
    reduce_scatter x1, waiting for transfers between devices, local(): lax.psum_scatter(jnp.stack([gate_part, up_part, back_part], axis=1).astyp...  41.3 us
    all_gather x1, waiting for transfers between devices, local(): lax.all_gather(jnp.concatenate([hidden, d_gate], axis=1), 'dp', axis=0, t...  30.9 us
    all_to_all x1, waiting for transfers between devices, local(): lax.all_to_all(send_x, 'expert', split_axis=0, concat_axis=0, tiled=True)  29.1 us
    all_to_all x1, waiting for transfers between devices, local(): lax.all_to_all(send_dy, 'expert', split_axis=0, concat_axis=0, tiled=True)  25.3 us
    all_to_all x1, waiting for transfers between devices, local(): lax.all_to_all(back, 'expert', split_axis=0, concat_axis=0, tiled=True)  24.8 us
    all_gather x1, waiting for transfers between devices, local(): up_part = lax.all_gather(d_up, 'dp', axis=0, tiled=True)  23.6 us
    dot_general x3, matrix products, contract_last(): lax.dot_general(left, right, (((1,), (1,)), ((), ())), preferred_element_...  19.6 us
    dot_general x2, matrix products, contract_first(): lax.dot_general(left, right, (((0,), (0,)), ((), ())), preferred_element_...  17.2 us
  transfers between devices with their start and end apart: 6, of which 6 were waited for; matrix products, arithmetic and copies ran while one was open for 14% of the time, Pallas kernels for 0%

profile of v1, /device:TPU:0, one launch (start us, length us, event | category | flops | bytes accessed | tf_op | source)
XLA Modules:
  0.0 294.6 jit_solution(3567743396176133277)
XLA Ops:
  7.2 0.8 fusion.50
  8.0 1.2 reduce-window.6
  9.4 0.8 fusion.49
  10.2 0.7 multiply_add_fusion
  10.9 2.7 convolution_convert_fusion.1
  13.6 4.1 %reshape.132 = bf16[32,20,1792]{2,1,0:T(8,128)(2,1)} reshape(bf16[640,1792]{1,0:T(8,128)(2,1)} %convolution_convert_fusion.1) | data formatting | bytes 4587520 | tf_op jit(solution)/shard_map/reshape | solution.py:61
  17.7 8.5 %all-to-all-start = ((bf16[32,20,1792]{2,1,0:T(8,128)(2,1)}), bf16[32,20,1792]{2,1,0:T(8,128)(2,1)S(1)}, u32[]{:S(2)}, u32[]{:S(2)}) async-start(bf16[32,20,1792]{2,1,0:T(8,128)(2,1)} %reshape.132), calls=%async_computation | async-start | bytes 5505024 | tf_op jit(solution)/shard_map/all_to_all | solution.py:64
  26.3 4.2 %convolution_convert_fusion = bf16[640,1792]{1,0:T(8,128)(2,1)} fusion(bf16[512,1792]{1,0:T(8,128)(2,1)} %param.9, f32[512]{0:T(512)S(1)} %bitcast.102, s32[512]{0:T(512)S(1)} %multiply_add_fusion), kind=kOutput, calls=%fused_computation.24 | convolution fusion | flops 1176207360 | bytes 4132864 | tf_op jit(solution)/shard_map/dot_general | solution.py:60
  30.6 4.1 %reshape.134 = bf16[32,20,1792]{2,1,0:T(8,128)(2,1)} reshape(bf16[640,1792]{1,0:T(8,128)(2,1)} %convolution_convert_fusion) | data formatting | bytes 4587520 | tf_op jit(solution)/shard_map/reshape | solution.py:62
  34.6 29.1 %all-to-all-done = bf16[32,20,1792]{2,1,0:T(8,128)(2,1)S(1)} async-done(((bf16[32,20,1792]{2,1,0:T(8,128)(2,1)}), bf16[32,20,1792]{2,1,0:T(8,128)(2,1)S(1)}, u32[]{:S(2)}, u32[]{:S(2)}) %all-to-all-start) | async-done | bytes 2293792 | tf_op jit(solution)/shard_map/all_to_all | solution.py:64
  63.8 4.8 %all-to-all-start.1 = ((bf16[32,20,1792]{2,1,0:T(8,128)(2,1)}), bf16[32,20,1792]{2,1,0:T(8,128)(2,1)}, u32[]{:S(2)}, u32[]{:S(2)}) async-start(bf16[32,20,1792]{2,1,0:T(8,128)(2,1)} %reshape.134), calls=%async_computation.1 | async-start | bytes 5505024 | tf_op jit(solution)/shard_map/all_to_all | solution.py:65
  68.6 2.1 reshape.133
  70.7 6.5 %fusion.31 = bf16[640,1,1024]{2,0,1:T(8,128)(2,1)} fusion(bf16[640,1792]{1,0:T(8,128)(2,1)} %reshape.133, bf16[1,1792,1024]{2,1,0:T(8,128)(2,1)} %param.13), kind=kOutput, calls=%fused_computation.31 | convolution fusion | flops 2349465600 | bytes 7274496 | tf_op jit(solution)/shard_map/dot_general | solution.py:74
  77.2 3.6 %fusion.34 = bf16[640,1,1024]{2,0,1:T(8,128)(2,1)} fusion(bf16[640,1792]{1,0:T(8,128)(2,1)S(1)} %copy-done.2, bf16[1,1792,1024]{2,1,0:T(8,128)(2,1)S(1)} %copy-done.6), kind=kOutput, calls=%fused_computation.32 | convolution fusion | flops 2349465600 | bytes 7274496 | tf_op jit(solution)/shard_map/dot_general | solution.py:73
  80.8 25.3 %all-to-all-done.1 = bf16[32,20,1792]{2,1,0:T(8,128)(2,1)} async-done(((bf16[32,20,1792]{2,1,0:T(8,128)(2,1)}), bf16[32,20,1792]{2,1,0:T(8,128)(2,1)}, u32[]{:S(2)}, u32[]{:S(2)}) %all-to-all-start.1) | async-done | bytes 2293792 | tf_op jit(solution)/shard_map/all_to_all | solution.py:65
  106.1 2.7 reshape.135
  108.8 4.7 %fusion.28 = bf16[640,1,1024]{2,0,1:T(8,128)(2,1)S(1)} fusion(bf16[640,1792]{1,0:T(8,128)(2,1)S(1)} %reshape.135, bf16[1,1024,1792]{2,1,0:T(8,128)(2,1)} %param.14), kind=kOutput, calls=%fused_computation.30 | convolution fusion | flops 2349465600 | bytes 7274496 | tf_op jit(solution)/shard_map/dot_general | solution.py:28
  113.6 2.1 pad_maximum_fusion
  115.7 41.3 %reduce-scatter.2.cloned.1.call-done = bf16[160,3,1024]{2,0,1:T(8,128)(2,1)} async-done(((bf16[640,3,1024]{2,0,1:T(8,128)(2,1)}), bf16[160,3,1024]{2,0,1:T(8,128)(2,1)}) %reduce-scatter.2.cloned.1.call-update) | async-done | bytes 983056 | tf_op jit(solution)/shard_map/reduce_scatter | solution.py:76
  157.1 1.4 convert_element_type.104
  158.5 1.2 multiply_convert_fusion.2
  159.9 0.9 pad_maximum_fusion.1
  160.8 23.6 %all-gather.5.cloned.1.call-done = bf16[640,1024]{1,0:T(8,128)(2,1)} async-done(((bf16[160,1024]{1,0:T(8,128)(2,1)}), bf16[640,1024]{1,0:T(8,128)(2,1)}) %all-gather.5.cloned.1.call-update) | async-done | bytes 1310736 | tf_op jit(solution)/shard_map/all_gather | solution.py:88
  184.5 7.1 %fusion.8 = f32[640,1792]{1,0:T(8,128)} fusion(bf16[640,1024]{1,0:T(8,128)(2,1)} %all-gather.5.cloned.1.call-done, bf16[1,1792,1024]{2,1,0:T(8,128)(2,1)} %param.13), kind=kOutput, calls=%fused_computation.14 | convolution fusion | flops 2348810240 | bytes 9568256 | tf_op jit(solution)/shard_map/dot_general | solution.py:28
  191.6 30.9 %all-gather.3.cloned.1.call-done = bf16[640,2048]{1,0:T(8,128)(2,1)} async-done(((bf16[160,2048]{1,0:T(8,128)(2,1)}), bf16[640,2048]{1,0:T(8,128)(2,1)}) %all-gather.3.cloned.1.call-update) | async-done | bytes 2621456 | tf_op jit(solution)/shard_map/all_gather | solution.py:84
  222.5 7.8 %add_convert_fusion = bf16[640,1792]{1,0:T(8,128)(2,1)} fusion(f32[640,1792]{1,0:T(8,128)} %fusion.8, bf16[1,1792,1024]{2,1,0:T(8,128)(2,1)} %param.12, bf16[640,2048]{1,0:T(8,128)(2,1)} %all-gather.3.cloned.1.call-done), kind=kOutput, calls=%fused_computation.10 | convolution fusion | flops 2351104000 | bytes 11862016 | tf_op jit(solution)/shard_map/dot_general | solution.py:28
  230.3 4.1 %reshape.136 = bf16[32,20,1792]{2,1,0:T(8,128)(2,1)} reshape(bf16[640,1792]{1,0:T(8,128)(2,1)} %add_convert_fusion) | data formatting | bytes 4587520 | tf_op jit(solution)/shard_map/reshape | solution.py:94
  234.4 7.4 %all-to-all-start.2 = ((bf16[32,20,1792]{2,1,0:T(8,128)(2,1)}), bf16[32,20,1792]{2,1,0:T(8,128)(2,1)}, u32[]{:S(2)}, u32[]{:S(2)}) async-start(bf16[32,20,1792]{2,1,0:T(8,128)(2,1)} %reshape.136), calls=%async_computation.3 | async-start | bytes 5505024 | tf_op jit(solution)/shard_map/all_to_all | solution.py:95
  241.8 12.7 %convert_bitcast_fusion = (bf16[1,1024,1792]{2,1,0:T(8,128)(2,1)}, bf16[1,1024,1792]{2,1,0:T(8,128)(2,1)}) fusion(bf16[1,1024,1792]{2,1,0:T(8,128)(2,1)} %param.14, bf16[640,1792]{1,0:T(8,128)(2,1)S(1)} %reshape.135, bf16[640,2048]{1,0:T(8,128)(2,1)} %all-gather.3.cloned.1.call-done, bf16[1,1024,1792]{2,1,0:T(8,128)(2,1)} %param.15), kind=kOutput, calls=%fused_computation.22 | convolution fusion | flops 2381840384 | bytes 18284544 | tf_op jit(solution)/shard_map/dot_general | solution.py:34
  254.5 24.8 %all-to-all-done.2 = bf16[32,20,1792]{2,1,0:T(8,128)(2,1)} async-done(((bf16[32,20,1792]{2,1,0:T(8,128)(2,1)}), bf16[32,20,1792]{2,1,0:T(8,128)(2,1)}, u32[]{:S(2)}, u32[]{:S(2)}) %all-to-all-start.2) | async-done | bytes 2293792 | tf_op jit(solution)/shard_map/all_to_all | solution.py:95
  279.3 4.3 %reshape.137 = bf16[640,1792]{1,0:T(8,128)(2,1)} reshape(bf16[32,20,1792]{2,1,0:T(8,128)(2,1)} %all-to-all-done.2) | data formatting | bytes 4587520 | tf_op jit(solution)/shard_map/reshape | solution.py:96
  283.5 4.5 %convolution_convert_fusion.2 = bf16[512,1792]{1,0:T(8,128)(2,1)} fusion(bf16[640,1792]{1,0:T(8,128)(2,1)} %reshape.137, s32[512]{0:T(512)S(1)} %multiply_add_fusion), kind=kOutput, calls=%fused_computation.26 | convolution fusion | flops 1176305664 | bytes 4130816 | tf_op jit(solution)/shard_map/dot_general | solution.py:34
  (24 shorter events, 0.7 us)
Async XLA Ops:
  7.2 3.7 %copy-start = (bf16[512,1792]{1,0:T(8,128)(2,1)S(1)}, bf16[512,1792]{1,0:T(8,128)(2,1)}, u32[]{:S(2)}) copy-start(bf16[512,1792]{1,0:T(8,128)(2,1)} %param.8) | copy-start | bytes 5505028
  17.7 8.6 %copy-start.5 = (s32[512,1]{0,1:T(1,128)S(1)}, s32[512,1]{0,1:T(1,128)}, u32[]{:S(2)}) copy-start(s32[512,1]{0,1:T(1,128)} %param.11) | copy-start | bytes 6148
  17.7 46.0 %all-to-all-start = ((bf16[32,20,1792]{2,1,0:T(8,128)(2,1)}), bf16[32,20,1792]{2,1,0:T(8,128)(2,1)S(1)}, u32[]{:S(2)}, u32[]{:S(2)}) async-start(bf16[32,20,1792]{2,1,0:T(8,128)(2,1)} %reshape.132), calls=%async_computation | async-start | bytes 5505024 | tf_op jit(solution)/shard_map/all_to_all | solution.py:64
  63.8 42.3 %all-to-all-start.1 = ((bf16[32,20,1792]{2,1,0:T(8,128)(2,1)}), bf16[32,20,1792]{2,1,0:T(8,128)(2,1)}, u32[]{:S(2)}, u32[]{:S(2)}) async-start(bf16[32,20,1792]{2,1,0:T(8,128)(2,1)} %reshape.134), calls=%async_computation.1 | async-start | bytes 5505024 | tf_op jit(solution)/shard_map/all_to_all | solution.py:65
  68.6 88.5 %reduce-scatter.2.cloned.1.call-start = ((), (), s32[]{:S(2)}) async-start(), calls=%async_computation.4 | async-start | bytes 4915200 | tf_op jit(solution)/shard_map/reduce_scatter | solution.py:76
  70.7 6.5 %copy-start.2 = (bf16[640,1792]{1,0:T(8,128)(2,1)S(1)}, bf16[640,1792]{1,0:T(8,128)(2,1)}, u32[]{:S(2)}) copy-start(bf16[640,1792]{1,0:T(8,128)(2,1)} %reshape.133) | copy-start | bytes 6881284
  70.7 6.5 %copy-start.6 = (bf16[1,1792,1024]{2,1,0:T(8,128)(2,1)S(1)}, bf16[1,1792,1024]{2,1,0:T(8,128)(2,1)}, u32[]{:S(2)}) copy-start(bf16[1,1792,1024]{2,1,0:T(8,128)(2,1)} %param.12) | copy-start | bytes 11010052
  108.8 4.8 %copy-start.3 = (bf16[640,1,1024]{2,0,1:T(8,128)(2,1)S(1)}, bf16[640,1,1024]{2,0,1:T(8,128)(2,1)}, u32[]{:S(2)}) copy-start(bf16[640,1,1024]{2,0,1:T(8,128)(2,1)} %fusion.31) | copy-start | bytes 3932164
  108.8 4.8 %copy-start.4 = (bf16[640,1,1024]{2,0,1:T(8,128)(2,1)S(1)}, bf16[640,1,1024]{2,0,1:T(8,128)(2,1)}, u32[]{:S(2)}) copy-start(bf16[640,1,1024]{2,0,1:T(8,128)(2,1)} %fusion.34) | copy-start | bytes 3932164
  115.7 68.8 %all-gather.5.cloned.1.call-start = ((), (), s32[]{:S(2)}) async-start(), calls=%async_computation.6 | async-start | bytes 1638400 | tf_op jit(solution)/shard_map/all_gather | solution.py:88
  159.7 62.8 %all-gather.3.cloned.1.call-start = ((), (), s32[]{:S(2)}) async-start(), calls=%async_computation.5 | async-start | bytes 3276800 | tf_op jit(solution)/shard_map/all_gather | solution.py:84
  234.4 44.9 %all-to-all-start.2 = ((bf16[32,20,1792]{2,1,0:T(8,128)(2,1)}), bf16[32,20,1792]{2,1,0:T(8,128)(2,1)}, u32[]{:S(2)}, u32[]{:S(2)}) async-start(bf16[32,20,1792]{2,1,0:T(8,128)(2,1)} %reshape.136), calls=%async_computation.3 | async-start | bytes 5505024 | tf_op jit(solution)/shard_map/all_to_all | solution.py:95
  279.3 8.8 %copy-start.1 = (bf16[512,1792]{1,0:T(8,128)(2,1)S(1)}, bf16[512,1792]{1,0:T(8,128)(2,1)}, u32[]{:S(2)}) copy-start(bf16[512,1792]{1,0:T(8,128)(2,1)} %param.8) | copy-start | bytes 5505028
Sparse Core Ops, SparseCore 0:
  115.8 41.2 reduce-scatter.1
  159.8 24.6 all-gather.4
  186.7 35.7 all-gather.2
